TPU v7x, 32 devices: a whole 2x2x4 slice. The times are simulated.
32 devices in a mesh: groups: 2 (over x), cache: 16 (over z, y, core).
Axes of the slice: x: 2, y: 2, z: 4, core: 2. Of those that a mesh axis runs over, the one named last changes fastest.
Arguments:
- prefix_len: int32 [32], P('groups'), parts along dimension 0, may hold values from 128 to 1024, as said below
- hits: int32 [32, 1], P('groups'), parts along dimension 0, may hold values from 0 to 15, as said below
- span_block: int32 [32, 16], P('groups'), parts along dimension 0, may hold values from 0 to 15, each once within a row
- queries: bfloat16 [2048, 2048], P(('groups', 'cache')), parts along dimension 0, may hold values from -100 to 100
- fresh_keys: bfloat16 [2048, 128], P(('groups', 'cache')), parts along dimension 0, may hold values from -4 to 4
- fresh_values: bfloat16 [2048, 128], P(('groups', 'cache')), parts along dimension 0, may hold values from -4 to 4
- cache_keys: bfloat16 [65536, 128], P(('groups', 'cache')), parts along dimension 0, may hold values from -4 to 4
- cache_values: bfloat16 [65536, 128], P(('groups', 'cache')), parts along dimension 0, may hold values from -4 to 4
Outputs:
- attended: bfloat16 [2048, 2048], P(('groups', 'cache')), parts along dimension 0
There are 2 independent parts, one for each index of `groups`. A program takes and returns all parts, laid end to end along the dimension named above; each array names one. Nothing has to cross between parts.
Inputs may be any that keep to these rules, and one draw needn't show every extreme that they name: `prefix_len`: every request's prefix holds at least 128 tokens, and one request in every draw holds exactly 1024. `hits`: each row names 1 different devices. Each device is named by at most 2 requests; 4 devices are named by exactly 2, half of them by one, a quarter by none. `span_block`: each row is a permutation.
All inputs are finite; a program needn't handle non-finite values.
Results may differ from a plain program's by a relative error of at most 0.0065.
Values may be sent and summed in bfloat16 or wider, within the bound.
A program may use at most 64 MiB of HBM per device.

v0:
```python
import math
import jax
import jax.numpy as jnp
from jax import lax
from jax.sharding import PartitionSpec as P

HEADS = 16
HD = 128
PAGE = 128
CAP = 2
REQUESTS = 16
TOK_REQ = 4
PAGES_DEV = 16
floor_score = -1e30


def owner_block(query_block, page_keys, page_values, visible):
    scale = HD ** (-0.5)
    scores = (
        jnp.einsum("thd,kd->thk", query_block, page_keys, preferred_element_type=jnp.float32)
        * scale
    )
    scores = jnp.where(visible, scores, floor_score)
    maxima = jnp.max(scores, axis=2)
    weights = jnp.exp(scores - maxima[:, :, None]) * visible
    totals = jnp.maximum(jnp.sum(weights, axis=2), 1.0)
    summed = jnp.einsum(
        "thk,kd->thd", weights.astype(jnp.bfloat16), page_values, preferred_element_type=jnp.float32
    )
    partial_out = (summed / totals[:, :, None]).astype(jnp.bfloat16)
    return (partial_out, maxima + jnp.log(totals))


def serve_slots(slot_queries, slot_keys, slot_values, slot_visible, devices):
    per_group = math.gcd(devices, 16)

    def one_slot(packed):
        queries_in, page_keys, page_values, visible = packed
        grouped = queries_in.reshape(devices // per_group, per_group * TOK_REQ, HEADS, HD)

        def one_group(query_block):
            return owner_block(query_block, page_keys, page_values, visible)

        outputs, lse_rows = lax.map(one_group, grouped)
        return (
            outputs.reshape(devices, TOK_REQ, HEADS * HD),
            lse_rows.reshape(devices, TOK_REQ, HEADS),
        )

    return lax.map(one_slot, (slot_queries, slot_keys, slot_values, slot_visible))


def body(prefix_len, hits, span_block, queries, fresh_keys, fresh_values, cache_keys, cache_values):
    devices = lax.axis_size("cache")
    myself = lax.axis_index("cache")
    hit_count = hits.shape[1]
    region = PAGES_DEV // CAP * PAGE
    per_device = REQUESTS * TOK_REQ
    scale = HD ** (-0.5)
    offsets = jnp.arange(TOK_REQ, dtype=jnp.int32)
    request_ids = jnp.arange(REQUESTS, dtype=jnp.int32)
    owner_ids = jnp.arange(devices, dtype=jnp.int32)
    slot_ids = jnp.arange(CAP, dtype=jnp.int32)
    is_named = jnp.any(hits[:, :, None] == owner_ids[None, None, :], axis=1).astype(jnp.int32)
    earlier = (request_ids[None, :] < request_ids[:, None]).astype(jnp.int32)
    slot_rank = jnp.sum(earlier[:, :, None] * is_named[None, :, :], axis=1)
    holding = (is_named[None] == 1) & (slot_rank[None] == slot_ids[:, None, None])
    occupied = jnp.any(holding, axis=1)
    send_request = jnp.sum(holding * request_ids[None, :, None], axis=1)
    local_request = jnp.take(send_request, myself, axis=1)
    local_occupied = jnp.take(occupied, myself, axis=1)
    local_hits = jnp.take(hits, local_request, axis=0)
    hit_place = jnp.sum(
        jnp.where(local_hits == myself, jnp.arange(hit_count, dtype=jnp.int32)[None, :], 0), axis=1
    )
    page_limit = jnp.take(prefix_len, local_request)
    prefix_spot = hit_place[:, None] * region + jnp.arange(region, dtype=jnp.int32)[None, :]
    slot_visible = local_occupied[:, None] & (prefix_spot < page_limit[:, None])
    region_keys = cache_keys.reshape(CAP, region, HD)
    region_values = cache_values.reshape(CAP, region, HD)
    query_heads = queries.reshape(REQUESTS, TOK_REQ, HEADS, HD)
    my_blocks = jnp.take(span_block, myself, axis=1)
    query_spot = my_blocks[:, None] * TOK_REQ + offsets[None, :]
    running = jnp.full((REQUESTS, TOK_REQ, HEADS), floor_score, jnp.float32)
    key_piece = lax.all_gather(fresh_keys, "cache", axis=0, tiled=True)
    value_piece = lax.all_gather(fresh_values, "cache", axis=0, tiled=True)
    count = key_piece.shape[0] // per_device
    key_rows = jnp.transpose(key_piece.reshape(count, REQUESTS, TOK_REQ, HD), (1, 0, 2, 3)).reshape(
        REQUESTS, count * TOK_REQ, HD
    )
    value_rows = jnp.transpose(
        value_piece.reshape(count, REQUESTS, TOK_REQ, HD), (1, 0, 2, 3)
    ).reshape(REQUESTS, count * TOK_REQ, HD)
    key_spot = (span_block[:, :, None] * TOK_REQ + offsets[None, None, :]).reshape(
        REQUESTS, count * TOK_REQ
    )
    visible = (key_spot[:, None, :] <= query_spot[:, :, None])[:, :, None, :]
    scores = (
        jnp.einsum("rthd,rkd->rthk", query_heads, key_rows, preferred_element_type=jnp.float32)
        * scale
    )
    scores = jnp.where(visible, scores, floor_score)
    highest = jnp.maximum(running, jnp.max(scores, axis=3))
    weights = jnp.exp(scores - highest[..., None]) * visible
    totals = jnp.sum(weights, axis=3)
    value_wide = value_rows.astype(jnp.float32)
    summed = jnp.einsum("rthk,rkd->rthd", weights, value_wide, precision=lax.Precision.HIGHEST)
    running, totals, summed = (highest, totals, summed)
    prompt_out = summed / totals[..., None]
    prompt_lse = running + jnp.log(totals)
    units = queries.reshape(REQUESTS, TOK_REQ, HEADS * HD)
    outgoing = jnp.take(units, send_request, axis=0)
    arrived_queries = lax.all_to_all(outgoing, "cache", split_axis=1, concat_axis=1, tiled=True)
    partial_out, partial_lse = serve_slots(
        arrived_queries, region_keys, region_values, slot_visible, devices
    )
    returned_out, returned_lse = (
        lax.all_to_all(
            partial_out.astype(jnp.float32), "cache", split_axis=1, concat_axis=1, tiled=True
        ).astype(partial_out.dtype),
        lax.all_to_all(partial_lse, "cache", split_axis=1, concat_axis=1, tiled=True),
    )
    flat_out = returned_out.reshape(CAP * devices, TOK_REQ, HEADS, HD)
    flat_lse = returned_lse.reshape(CAP * devices, TOK_REQ, HEADS)
    hit_rank = jnp.take_along_axis(slot_rank, hits, axis=1)
    source = hit_rank * devices + hits
    owner_out = jnp.take(flat_out, source, axis=0)
    owner_lse = jnp.take(flat_lse, source, axis=0)
    every_lse = jnp.concatenate([prompt_lse[:, None], owner_lse], axis=1)
    highest = jnp.max(every_lse, axis=1)
    shares = jnp.exp(every_lse - highest[:, None])
    combined = shares[:, 0, :, :, None] * prompt_out + jnp.einsum(
        "rith,rithd->rthd", shares[:, 1:], owner_out, preferred_element_type=jnp.float32
    )
    result = combined / jnp.sum(shares, axis=1)[..., None]
    return result.astype(jnp.bfloat16).reshape(per_device, HEADS * HD)


def solution(mesh):
    in_specs = (
        P("groups"),
        P("groups", None),
        P("groups", None),
        P(("groups", "cache"), None),
        P(("groups", "cache"), None),
        P(("groups", "cache"), None),
        P(("groups", "cache"), None),
        P(("groups", "cache"), None),
    )
    out_specs = P(("groups", "cache"), None)
    return jax.shard_map(body, mesh=mesh, in_specs=in_specs, out_specs=out_specs, check_vma=False)
```

profile of v0, /device:TPU:0, one launch (start us, length us, event | category | flops | bytes accessed | tf_op | source)
XLA Modules:
  0.0 96.3 jit_solution(12392458391359597815)
XLA Ops:
  0.0 0.8 broadcast_compare_fusion.1
  1.1 1.1 %reshape.331 = bf16[16,4,2048]{2,1,0:T(4,128)(2,1)S(1)} reshape(bf16[64,2048]{1,0:T(8,128)(2,1)} %param.13) | data formatting | bytes 524288 | tf_op jit(solution)/shard_map/reshape | solution.py:111
  2.1 1.0 %gather_fusion.1 = bf16[32,4,2048]{2,1,0:T(4,128)(2,1)S(1)} fusion(bf16[16,4,2048]{2,1,0:T(4,128)(2,1)S(1)} %reshape.331, s32[1024]{0:T(1024)S(1)} %pad_clamp_fusion.1), kind=kCustom, calls=%fused_computation.1 | custom fusion | bytes 1048704 | tf_op jit(solution)/shard_map/jit(_take)/gather | solution.py:112
  3.2 0.3 copy.71
  3.6 1.2 %copy.72 = bf16[2,16,4,2048]{3,2,0,1:T(4,128)(2,1)} copy(bf16[2,16,4,2048]{3,1,0,2:T(8,128)(2,1)S(1)} %broadcast_select_fusion) | data formatting | bytes 1048576 | tf_op jit(solution)/shard_map/jit(_take)/select_n | solution.py:112
  4.8 7.4 %all-to-all-start = ((bf16[2,16,4,2048]{3,2,0,1:T(4,128)(2,1)}), bf16[2,16,4,2048]{3,2,0,1:T(4,128)(2,1)S(1)}, u32[]{:S(2)}, u32[]{:S(2)}) async-start(bf16[2,16,4,2048]{3,2,0,1:T(4,128)(2,1)} %copy.72), calls=%async_computation | async-start | bytes 1048576 | tf_op jit(solution)/shard_map/all_to_all | solution.py:113
  12.5 0.2 select_reduce_fusion.1
  12.7 0.7 gather_fusion.4
  13.9 24.2 %all_gather.6 = bf16[1024,128]{1,0:T(8,128)(2,1)S(1)} all-gather(bf16[64,128]{1,0:T(8,128)(2,1)S(1)} %copy-done.4), channel_id=1, replica_groups=mesh['groups'=2,'cache'=16] {'cache'}, dimensions={0}, use_global_device_ids=true | all-gather | bytes 278528 | tf_op jit(solution)/shard_map/all_gather | solution.py:85
  38.3 0.6 gather_fusion
  39.0 0.4 fusion.43
  39.4 0.4 fusion.26
  40.0 7.6 %while.20 = (s32[]{:T(128)}, bf16[2,16,4,2048]{3,1,2,0:T(8,128)(2,1)S(1)}, f32[2,16,4,16]{3,2,0,1:T(4,128)S(1)}, pred[2,1024]{1,0:T(4,128)(4,1)S(1)}, bf16[2,16,...) while((s32[]{:T(128)}, ...), condition=%wide.region_8.9_spmd, body=%wide.region_5.0_spmd.sunk | while | flops 550765568 | bytes 15906925 | solution.py:50
  40.3 0.8 fusion.57
  41.1 1.2 %fusion.58 = f32[64,16]{1,0:T(8,128)S(1)} fusion(f32[64,16,1024]{2,1,0:T(8,128)S(1)} %get-tuple-element.216, f32[1024]{0:T(1024)S(1)} %convert_element_type.76, f32[64,16]{1,0:T(8,128)S(1)} %get-tuple-element.217, pred[1024]{0:T(1024)(128)(4,1)S(1)} %dynamic-slice_reduce_fusion.2), kind=kLoop, calls=%fused_computation.8.clone.1 | loop fusion | flops 5241856 | bytes 4207616 | tf_op jit(solution)/shard_map/while/body/eval_jaxpr/while/body/eval_jaxpr/reduce_sum | solution.py:26
  42.3 1.1 %fusion.59 = bf16[64,16,128]{2,1,0:T(8,128)(2,1)S(1)} fusion(f32[64,16,1024]{2,1,0:T(8,128)S(1)} %get-tuple-element.216, f32[1024]{0:T(1024)S(1)} %convert_element_type.76, f32[64,16]{1,0:T(8,128)S(1)} %get-tuple-element.217, pred[1024]{0:T(1024)(128)(4,1)S(1)} %dynamic-slice_reduce_fusion.2, f32[64,16]{1,0:T(8,128)S(1)} %get-tuple-element.218, ...), kind=kOutput, calls=%fused_computation.13.clone.1 | convolution fusion | flops 273940480 | bytes 4789252 | tf_op jit(solution)/shard_map/while/body/eval_jaxpr/while/body/eval_jaxpr/thk,kd->thd/dot_general | solution.py:27
  44.1 0.8 fusion.57
  44.9 1.2 %fusion.58 = f32[64,16]{1,0:T(8,128)S(1)} fusion(f32[64,16,1024]{2,1,0:T(8,128)S(1)} %get-tuple-element.216, f32[1024]{0:T(1024)S(1)} %convert_element_type.76, f32[64,16]{1,0:T(8,128)S(1)} %get-tuple-element.217, pred[1024]{0:T(1024)(128)(4,1)S(1)} %dynamic-slice_reduce_fusion.2), kind=kLoop, calls=%fused_computation.8.clone.1 | loop fusion | flops 5241856 | bytes 4207616 | tf_op jit(solution)/shard_map/while/body/eval_jaxpr/while/body/eval_jaxpr/reduce_sum | solution.py:26
  46.1 1.1 %fusion.59 = bf16[64,16,128]{2,1,0:T(8,128)(2,1)S(1)} fusion(f32[64,16,1024]{2,1,0:T(8,128)S(1)} %get-tuple-element.216, f32[1024]{0:T(1024)S(1)} %convert_element_type.76, f32[64,16]{1,0:T(8,128)S(1)} %get-tuple-element.217, pred[1024]{0:T(1024)(128)(4,1)S(1)} %dynamic-slice_reduce_fusion.2, f32[64,16]{1,0:T(8,128)S(1)} %get-tuple-element.218, ...), kind=kOutput, calls=%fused_computation.13.clone.1 | convolution fusion | flops 273940480 | bytes 4789252 | tf_op jit(solution)/shard_map/while/body/eval_jaxpr/while/body/eval_jaxpr/thk,kd->thd/dot_general | solution.py:27
  47.5 0.7 reshape.490
  48.3 3.5 %all-to-all-start.1 = ((f32[16,1,128]{2,1,0:T(1,128)}), f32[16,1,128]{2,1,0:T(1,128)S(1)}, u32[]{:S(2)}, u32[]{:S(2)}) async-start(f32[16,1,128]{2,1,0:T(1,128)} %reshape.490), calls=%async_computation.1 | async-start | bytes 16384 | tf_op jit(solution)/shard_map/all_to_all | solution.py:121
  51.7 22.4 %all_gather.7 = bf16[1024,128]{1,0:T(8,128)(2,1)S(1)} all-gather(bf16[64,128]{1,0:T(8,128)(2,1)S(1)} %copy-done.5), channel_id=1, replica_groups=mesh['groups'=2,'cache'=16] {'cache'}, dimensions={0}, use_global_device_ids=true | all-gather | bytes 278528 | tf_op jit(solution)/shard_map/all_gather | solution.py:86
  74.3 1.2 %copy.79 = bf16[2,16,4,2048]{3,2,0,1:T(4,128)(2,1)} copy(bf16[2,16,4,2048]{3,1,2,0:T(8,128)(2,1)S(1)} %get-tuple-element.65) | data formatting | bytes 1048576 | tf_op jit(solution)/shard_map/convert_element_type | solution.py:119
  75.5 3.6 %all-to-all-start.2 = ((bf16[2,16,4,2048]{3,2,0,1:T(4,128)(2,1)}), bf16[2,16,4,2048]{3,2,0,1:T(4,128)(2,1)S(1)}, u32[]{:S(2)}, u32[]{:S(2)}) async-start(bf16[2,16,4,2048]{3,2,0,1:T(4,128)(2,1)} %copy.79), calls=%async_computation.2 | async-start | bytes 1048576 | tf_op jit(solution)/shard_map/all_to_all | solution.py:118
  79.1 0.5 broadcast.506
  79.6 0.7 reduce.10
  80.4 0.6 gather_fusion.2
  81.2 12.3 %all-to-all-done.2 = bf16[2,16,4,2048]{3,2,0,1:T(4,128)(2,1)S(1)} async-done(((bf16[2,16,4,2048]{3,2,0,1:T(4,128)(2,1)}), bf16[2,16,4,2048]{3,2,0,1:T(4,128)(2,1)S(1)}, u32[]{:S(2)}, u32[]{:S(2)}) %all-to-all-start.2) | async-done | bytes 524320 | tf_op jit(solution)/shard_map/all_to_all | solution.py:118
  93.5 0.3 copy.80
  93.9 0.6 gather_fusion.3
  94.5 1.0 %fusion.25 = bf16[16,4,16,128]{3,2,1,0:T(8,128)(2,1)S(1)} fusion(bf16[16,64,128,1]{2,1,3,0:T(8,128)(2,1)S(1)} %bitcast.106, f32[16,4,16,64]{3,2,1,0:T(8,128)S(1)} %get-tuple-element.167, f32[16,4,16]{2,1,0:T(4,128)S(1)} %get-tuple-element.150, bf16[16,4,16,128]{3,2,1,0:T(8,128)(2,1)S(1)} %gather_fusion.3, f32[16,4,16]{2,1,0:T(4,128)S(1)} %get-tuple-element.161, ...), kind=kOutput, calls=%fused_computation.35 | convolution fusion | flops 101842944 | bytes 1085456 | tf_op jit(solution)/shard_map/rthk,rkd->rthd/dot_general | solution.py:107
  95.5 0.8 copy.98
  (77 shorter events, 3.3 us)
Async XLA Ops:
  0.0 38.2 %copy-start = (s32[16]{0:T(128)S(1)}, s32[16]{0:T(128)}, u32[]{:S(2)}) copy-start(s32[16]{0:T(128)} %param.10) | copy-start | bytes 196
  0.0 12.2 %copy-start.6 = (s32[16,1]{0,1:T(1,128)S(1)}, s32[16,1]{0,1:T(1,128)}, u32[]{:S(2)}) copy-start(s32[16,1]{0,1:T(1,128)} %param.11) | copy-start | bytes 196
  0.0 38.2 %copy-start.2 = (bf16[64,2048]{1,0:T(8,128)(2,1)S(1)}, bf16[64,2048]{1,0:T(8,128)(2,1)}, u32[]{:S(2)}) copy-start(bf16[64,2048]{1,0:T(8,128)(2,1)} %param.13) | copy-start | bytes 786436
  0.0 12.2 %copy-start.3 = (s32[16,16]{1,0:T(8,128)S(1)}, s32[16,16]{1,0:T(8,128)}, u32[]{:S(2)}) copy-start(s32[16,16]{1,0:T(8,128)} %param.12) | copy-start | bytes 3076
  0.0 13.9 %copy-start.4 = (bf16[64,128]{1,0:T(8,128)(2,1)S(1)}, bf16[64,128]{1,0:T(8,128)(2,1)}, u32[]{:S(2)}) copy-start(bf16[64,128]{1,0:T(8,128)(2,1)} %param.14) | copy-start | bytes 49156
  3.1 36.8 %copy-start.1 = (bf16[2048,128]{1,0:T(8,128)(2,1)S(1)}, bf16[2048,128]{1,0:T(8,128)(2,1)}, u32[]{:S(2)}) copy-start(bf16[2048,128]{1,0:T(8,128)(2,1)} %param.16) | copy-start | bytes 1572868
  3.1 36.8 %copy-start.7 = (bf16[2048,128]{1,0:T(8,128)(2,1)S(1)}, bf16[2048,128]{1,0:T(8,128)(2,1)}, u32[]{:S(2)}) copy-start(bf16[2048,128]{1,0:T(8,128)(2,1)} %param.17) | copy-start | bytes 1572868
  4.8 35.2 %all-to-all-start = ((bf16[2,16,4,2048]{3,2,0,1:T(4,128)(2,1)}), bf16[2,16,4,2048]{3,2,0,1:T(4,128)(2,1)S(1)}, u32[]{:S(2)}, u32[]{:S(2)}) async-start(bf16[2,16,4,2048]{3,2,0,1:T(4,128)(2,1)} %copy.72), calls=%async_computation | async-start | bytes 1048576 | tf_op jit(solution)/shard_map/all_to_all | solution.py:113
  40.0 11.8 %copy-start.5 = (bf16[64,128]{1,0:T(8,128)(2,1)S(1)}, bf16[64,128]{1,0:T(8,128)(2,1)}, u32[]{:S(2)}) copy-start(bf16[64,128]{1,0:T(8,128)(2,1)} %param.15) | copy-start | bytes 49156
  48.3 27.2 %all-to-all-start.1 = ((f32[16,1,128]{2,1,0:T(1,128)}), f32[16,1,128]{2,1,0:T(1,128)S(1)}, u32[]{:S(2)}, u32[]{:S(2)}) async-start(f32[16,1,128]{2,1,0:T(1,128)} %reshape.490), calls=%async_computation.1 | async-start | bytes 16384 | tf_op jit(solution)/shard_map/all_to_all | solution.py:121
  75.5 18.0 %all-to-all-start.2 = ((bf16[2,16,4,2048]{3,2,0,1:T(4,128)(2,1)}), bf16[2,16,4,2048]{3,2,0,1:T(4,128)(2,1)S(1)}, u32[]{:S(2)}, u32[]{:S(2)}) async-start(bf16[2,16,4,2048]{3,2,0,1:T(4,128)(2,1)} %copy.79), calls=%async_computation.2 | async-start | bytes 1048576 | tf_op jit(solution)/shard_map/all_to_all | solution.py:118
where the time goes:
time: 96.7 us; the launch traced here: 96.3 us
  blocking collectives  46.6 us (48%)
  starting transfers between devices  14.4 us (15%)
  waiting for transfers between devices  12.3 us (13%)
  local copies, waits for them, and re-layouts  11.6 us (12%)
  other arithmetic  5.59 us (6%)
  matrix products  5.26 us (5%)
    all_gather x1, blocking collectives, body(): key_piece = lax.all_gather(fresh_keys, 'cache', axis=0, tiled=True)  24.2 us
    all_gather x1, blocking collectives, body(): value_piece = lax.all_gather(fresh_values, 'cache', axis=0, tiled=True)  22.4 us
    all_to_all x1, waiting for transfers between devices, body(): lax.all_to_all(partial_out.astype(jnp.float32), 'cache', split_axis=1, co...  12.3 us
    all_to_all x1, starting transfers between devices, body(): lax.all_to_all(outgoing, 'cache', split_axis=1, concat_axis=1, tiled=True)  7.38 us
    all_to_all x1, starting transfers between devices, body(): lax.all_to_all(partial_out.astype(jnp.float32), 'cache', split_axis=1, co...  3.57 us
    all_to_all x1, starting transfers between devices, body(): lax.all_to_all(partial_lse, 'cache', split_axis=1, concat_axis=1, tiled=T...  3.47 us
    reduce_sum x2, other arithmetic, owner_block(): totals = jnp.maximum(jnp.sum(weights, axis=2), 1.0)  2.34 us
    dot_general x2, matrix products, owner_block(): jnp.einsum('thk,kd->thd', weights.astype(jnp.bfloat16), page_values, pref...  2.27 us
  transfers between devices with their start and end apart: 3, of which 1 were waited for; matrix products, arithmetic and copies ran while one was open for 7% of the time, Pallas kernels for 0%

commit v1 on v0

--- a/solution.py
+++ b/solution.py
@@ -115,8 +115,16 @@
         arrived_queries, region_keys, region_values, slot_visible, devices
     )
     returned_out, returned_lse = (
-        lax.all_to_all(
-            partial_out.astype(jnp.float32), "cache", split_axis=1, concat_axis=1, tiled=True
+        jnp.concatenate(
+            lax.all_to_all(
+                jnp.stack(
+                    jnp.split(partial_out.astype(jnp.float32), lax.axis_size("cache"), axis=1)
+                ),
+                "cache",
+                0,
+                0,
+            ),
+            axis=1,
         ).astype(partial_out.dtype),
         lax.all_to_all(partial_lse, "cache", split_axis=1, concat_axis=1, tiled=True),
     )

time: 96.7 us -> 105 us (1.086)
  other arithmetic: 5.59 us -> 9.79 us
  local copies, waits for them, and re-layouts: 11.6 us -> 15.5 us
  blocking collectives: 46.6 us -> 43.8 us
  starting transfers between devices: 14.4 us -> 16.8 us
    unnamed x0 -> x1, other arithmetic: none -> 4.2 us
    unnamed x23 -> x39, local copies, waits for them, and re-layouts: 1.85 us -> 5.45 us
    all_gather x1, blocking collectives: 22.4 us -> 19.7 us  [body(): value_piece = lax.all_gather(fresh_values, 'cache', axis=0, tiled=True)]
    all_to_all x1, starting transfers between devices: 3.57 us -> 5.79 us  [body(): lax.all_to_all(jnp.stack(jnp.split(partial_out.astype(jnp.float32), lax.a...]
  transfers between devices with their start and end apart: 3 -> 3, of which waited for: 1 -> 1; matrix products, arithmetic and copies ran while one was open for 7% -> 11% of each run, Pallas kernels for 0% -> 0%
where the time goes in v1:
time: 105 us; the launch traced here: 104 us
  blocking collectives  43.8 us (42%)
  starting transfers between devices  16.8 us (16%)
  local copies, waits for them, and re-layouts  15.5 us (15%)
  waiting for transfers between devices  12.3 us (12%)
  other arithmetic  9.79 us (9%)
  matrix products  5.26 us (5%)
    all_gather x1, blocking collectives, body(): key_piece = lax.all_gather(fresh_keys, 'cache', axis=0, tiled=True)  24.2 us
    all_gather x1, blocking collectives, body(): value_piece = lax.all_gather(fresh_values, 'cache', axis=0, tiled=True)  19.7 us
    all_to_all x1, waiting for transfers between devices, body(): lax.all_to_all(jnp.stack(jnp.split(partial_out.astype(jnp.float32), lax.a...  12.3 us
    all_to_all x1, starting transfers between devices, body(): lax.all_to_all(outgoing, 'cache', split_axis=1, concat_axis=1, tiled=True)  7.4 us
    all_to_all x1, starting transfers between devices, body(): lax.all_to_all(jnp.stack(jnp.split(partial_out.astype(jnp.float32), lax.a...  5.79 us
    unnamed x39, local copies, waits for them, and re-layouts  5.45 us
    unnamed x1, other arithmetic  4.2 us
    all_to_all x1, starting transfers between devices, body(): lax.all_to_all(partial_lse, 'cache', split_axis=1, concat_axis=1, tiled=T...  3.65 us
  transfers between devices with their start and end apart: 3, of which 1 were waited for; matrix products, arithmetic and copies ran while one was open for 11% of the time, Pallas kernels for 0%

profile of v1, /device:TPU:0, one launch (start us, length us, event | category | flops | bytes accessed | tf_op | source)
XLA Modules:
  0.0 104.1 jit_solution(12162634488042017397)
XLA Ops:
  0.0 0.8 broadcast_compare_fusion.1
  1.1 1.1 %reshape.333 = bf16[16,4,2048]{2,1,0:T(4,128)(2,1)S(1)} reshape(bf16[64,2048]{1,0:T(8,128)(2,1)} %param.13) | data formatting | bytes 524288 | tf_op jit(solution)/shard_map/reshape | solution.py:111
  2.1 1.0 gather_fusion.1
  3.6 1.2 %copy.160 = bf16[2,16,4,2048]{3,2,0,1:T(4,128)(2,1)} copy(bf16[2,16,4,2048]{3,1,0,2:T(8,128)(2,1)S(1)} %broadcast_select_fusion) | data formatting | bytes 1048576 | tf_op jit(solution)/shard_map/jit(_take)/select_n | solution.py:112
  4.8 7.4 %all-to-all-start = ((bf16[2,16,4,2048]{3,2,0,1:T(4,128)(2,1)}), bf16[2,16,4,2048]{3,2,0,1:T(4,128)(2,1)S(1)}, u32[]{:S(2)}, u32[]{:S(2)}) async-start(bf16[2,16,4,2048]{3,2,0,1:T(4,128)(2,1)} %copy.160), calls=%async_computation | async-start | bytes 1048576 | tf_op jit(solution)/shard_map/all_to_all | solution.py:113
  12.8 0.7 gather_fusion.4
  13.9 24.2 %all_gather.6 = bf16[1024,128]{1,0:T(8,128)(2,1)S(1)} all-gather(bf16[64,128]{1,0:T(8,128)(2,1)S(1)} %copy-done.4), channel_id=1, replica_groups=mesh['groups'=2,'cache'=16] {'cache'}, dimensions={0}, use_global_device_ids=true | all-gather | bytes 278528 | tf_op jit(solution)/shard_map/all_gather | solution.py:85
  38.3 19.7 %all_gather.7 = bf16[1024,128]{1,0:T(8,128)(2,1)S(1)} all-gather(bf16[64,128]{1,0:T(8,128)(2,1)S(1)} %copy-done.5), channel_id=1, replica_groups=mesh['groups'=2,'cache'=16] {'cache'}, dimensions={0}, use_global_device_ids=true | all-gather | bytes 278528 | tf_op jit(solution)/shard_map/all_gather | solution.py:86
  58.1 0.6 gather_fusion
  59.8 7.6 %while.20 = (s32[]{:T(128)}, bf16[2,16,4,2048]{3,1,2,0:T(8,128)(2,1)S(1)}, f32[2,16,4,16]{3,2,0,1:T(4,128)S(1)}, pred[2,1024]{1,0:T(4,128)(4,1)S(1)}, bf16[2,16,...) while((s32[]{:T(128)}, ...), condition=%wide.region_8.9_spmd, body=%wide.region_5.0_spmd.sunk | while | flops 550765568 | bytes 18004104 | solution.py:50
  60.1 0.8 fusion.73
  61.0 1.2 %fusion.74 = f32[64,16]{1,0:T(8,128)S(1)} fusion(f32[64,16,1024]{2,1,0:T(8,128)S(1)} %get-tuple-element.216, f32[1024]{0:T(1024)S(1)} %convert_element_type.86, f32[64,16]{1,0:T(8,128)S(1)} %get-tuple-element.217, pred[1024]{0:T(1024)(128)(4,1)S(1)} %dynamic-slice_reduce_fusion.2), kind=kLoop, calls=%fused_computation.8.clone.1 | loop fusion | flops 5241856 | bytes 4207616 | tf_op jit(solution)/shard_map/while/body/eval_jaxpr/while/body/eval_jaxpr/reduce_sum | solution.py:26
  62.2 1.1 %fusion.75 = bf16[64,16,128]{2,1,0:T(8,128)(2,1)S(1)} fusion(f32[64,16,1024]{2,1,0:T(8,128)S(1)} %get-tuple-element.216, f32[1024]{0:T(1024)S(1)} %convert_element_type.86, f32[64,16]{1,0:T(8,128)S(1)} %get-tuple-element.217, pred[1024]{0:T(1024)(128)(4,1)S(1)} %dynamic-slice_reduce_fusion.2, f32[64,16]{1,0:T(8,128)S(1)} %get-tuple-element.218, ...), kind=kOutput, calls=%fused_computation.13.clone.1 | convolution fusion | flops 273940480 | bytes 4789252 | tf_op jit(solution)/shard_map/while/body/eval_jaxpr/while/body/eval_jaxpr/thk,kd->thd/dot_general | solution.py:27
  63.9 0.8 fusion.73
  64.8 1.2 %fusion.74 = f32[64,16]{1,0:T(8,128)S(1)} fusion(f32[64,16,1024]{2,1,0:T(8,128)S(1)} %get-tuple-element.216, f32[1024]{0:T(1024)S(1)} %convert_element_type.86, f32[64,16]{1,0:T(8,128)S(1)} %get-tuple-element.217, pred[1024]{0:T(1024)(128)(4,1)S(1)} %dynamic-slice_reduce_fusion.2), kind=kLoop, calls=%fused_computation.8.clone.1 | loop fusion | flops 5241856 | bytes 4207616 | tf_op jit(solution)/shard_map/while/body/eval_jaxpr/while/body/eval_jaxpr/reduce_sum | solution.py:26
  66.0 1.1 %fusion.75 = bf16[64,16,128]{2,1,0:T(8,128)(2,1)S(1)} fusion(f32[64,16,1024]{2,1,0:T(8,128)S(1)} %get-tuple-element.216, f32[1024]{0:T(1024)S(1)} %convert_element_type.86, f32[64,16]{1,0:T(8,128)S(1)} %get-tuple-element.217, pred[1024]{0:T(1024)(128)(4,1)S(1)} %dynamic-slice_reduce_fusion.2, f32[64,16]{1,0:T(8,128)S(1)} %get-tuple-element.218, ...), kind=kOutput, calls=%fused_computation.13.clone.1 | convolution fusion | flops 273940480 | bytes 4789252 | tf_op jit(solution)/shard_map/while/body/eval_jaxpr/while/body/eval_jaxpr/thk,kd->thd/dot_general | solution.py:27
  68.6 0.7 reshape.491
  69.3 3.7 %all-to-all-start.1 = ((f32[16,1,128]{2,1,0:T(1,128)}), f32[16,1,128]{2,1,0:T(1,128)S(1)}, u32[]{:S(2)}, u32[]{:S(2)}) async-start(f32[16,1,128]{2,1,0:T(1,128)} %reshape.491), calls=%async_computation.1 | async-start | bytes 16384 | tf_op jit(solution)/shard_map/all_to_all | solution.py:129
  73.1 0.6 broadcast.507
  73.7 4.2 %reduce.11 = bf16[16,2,4,2048]{3,2,1,0:T(4,128)(2,1)S(1)} reduce(bf16[16,2,4,1,2048]{4,3,2,1,0:T(2,128)(2,1)S(1)} %bitcast.171, bf16[]{:T(256)} %broadcast.507), dimensions={3}, to_apply=%bitcast.145.reduce_sub_computation | reduce | bytes 1048578
  77.9 1.3 %reshape.493 = bf16[16,2,8192]{2,1,0:T(2,128)(2,1)} reshape(bf16[16,2,4,2048]{3,2,1,0:T(4,128)(2,1)S(1)} %reduce.11) | data formatting | bytes 1048576
  79.2 5.8 %all-to-all-start.2 = ((bf16[16,2,8192]{2,1,0:T(2,128)(2,1)}), bf16[16,2,8192]{2,1,0:T(2,128)(2,1)S(1)}, u32[]{:S(2)}, u32[]{:S(2)}) async-start(bf16[16,2,8192]{2,1,0:T(2,128)(2,1)} %reshape.493), calls=%async_computation.2 | async-start | bytes 1048576 | tf_op jit(solution)/shard_map/all_to_all | solution.py:119
  85.0 0.5 broadcast.506
  85.5 0.7 reduce.10
  86.3 0.6 gather_fusion.2
  87.2 12.3 %all-to-all-done.2 = bf16[16,2,8192]{2,1,0:T(2,128)(2,1)S(1)} async-done(((bf16[16,2,8192]{2,1,0:T(2,128)(2,1)}), bf16[16,2,8192]{2,1,0:T(2,128)(2,1)S(1)}, u32[]{:S(2)}, u32[]{:S(2)}) %all-to-all-start.2) | async-done | bytes 524320 | tf_op jit(solution)/shard_map/all_to_all | solution.py:119
  99.5 0.5 reshape.494
  100.0 1.1 %bitcast_bitcast_fusion = bf16[2,16,1,4,2048]{4,2,3,0,1:T(2,128)(2,1)S(1)} fusion(bf16[16,2,4,1,2048]{4,3,2,1,0:T(2,128)(2,1)S(1)} %reshape.494), kind=kLoop, calls=%fused_computation.126 | loop fusion | bytes 1048576 | tf_op jit(solution)/shard_map/convert_element_type | solution.py:128
  101.1 0.6 copy.167
  101.8 0.6 gather_fusion.3
  102.4 1.0 fusion.25
  103.4 0.8 copy.185
  (99 shorter events, 5.8 us)
Async XLA Ops:
  0.0 58.1 %copy-start = (s32[16]{0:T(128)S(1)}, s32[16]{0:T(128)}, u32[]{:S(2)}) copy-start(s32[16]{0:T(128)} %param.10) | copy-start | bytes 196
  0.0 12.2 %copy-start.6 = (s32[16,1]{0,1:T(1,128)S(1)}, s32[16,1]{0,1:T(1,128)}, u32[]{:S(2)}) copy-start(s32[16,1]{0,1:T(1,128)} %param.11) | copy-start | bytes 196
  0.0 38.2 %copy-start.2 = (bf16[64,2048]{1,0:T(8,128)(2,1)S(1)}, bf16[64,2048]{1,0:T(8,128)(2,1)}, u32[]{:S(2)}) copy-start(bf16[64,2048]{1,0:T(8,128)(2,1)} %param.13) | copy-start | bytes 786436
  0.0 12.2 %copy-start.3 = (s32[16,16]{1,0:T(8,128)S(1)}, s32[16,16]{1,0:T(8,128)}, u32[]{:S(2)}) copy-start(s32[16,16]{1,0:T(8,128)} %param.12) | copy-start | bytes 3076
  0.0 13.9 %copy-start.4 = (bf16[64,128]{1,0:T(8,128)(2,1)S(1)}, bf16[64,128]{1,0:T(8,128)(2,1)}, u32[]{:S(2)}) copy-start(bf16[64,128]{1,0:T(8,128)(2,1)} %param.14) | copy-start | bytes 49156
  0.0 38.3 %copy-start.5 = (bf16[64,128]{1,0:T(8,128)(2,1)S(1)}, bf16[64,128]{1,0:T(8,128)(2,1)}, u32[]{:S(2)}) copy-start(bf16[64,128]{1,0:T(8,128)(2,1)} %param.15) | copy-start | bytes 49156
  3.4 56.3 %copy-start.1 = (bf16[2048,128]{1,0:T(8,128)(2,1)S(1)}, bf16[2048,128]{1,0:T(8,128)(2,1)}, u32[]{:S(2)}) copy-start(bf16[2048,128]{1,0:T(8,128)(2,1)} %param.16) | copy-start | bytes 1572868
  4.8 55.0 %all-to-all-start = ((bf16[2,16,4,2048]{3,2,0,1:T(4,128)(2,1)}), bf16[2,16,4,2048]{3,2,0,1:T(4,128)(2,1)S(1)}, u32[]{:S(2)}, u32[]{:S(2)}) async-start(bf16[2,16,4,2048]{3,2,0,1:T(4,128)(2,1)} %copy.160), calls=%async_computation | async-start | bytes 1048576 | tf_op jit(solution)/shard_map/all_to_all | solution.py:113
  60.1 2.1 %copy-start.7 = (bf16[2,1024,128]{2,1,0:T(8,128)(2,1)S(1)}, bf16[2,1024,128]{2,1,0:T(8,128)(2,1)}, u32[]{:S(2)}) copy-start(bf16[2,1024,128]{2,1,0:T(8,128)(2,1)} %get-tuple-element.242) | copy-start | bytes 1572868 | tf_op jit(solution)/shard_map/while
  63.9 2.1 %copy-start.7 = (bf16[2,1024,128]{2,1,0:T(8,128)(2,1)S(1)}, bf16[2,1024,128]{2,1,0:T(8,128)(2,1)}, u32[]{:S(2)}) copy-start(bf16[2,1024,128]{2,1,0:T(8,128)(2,1)} %get-tuple-element.242) | copy-start | bytes 1572868 | tf_op jit(solution)/shard_map/while
  69.3 9.9 %all-to-all-start.1 = ((f32[16,1,128]{2,1,0:T(1,128)}), f32[16,1,128]{2,1,0:T(1,128)S(1)}, u32[]{:S(2)}, u32[]{:S(2)}) async-start(f32[16,1,128]{2,1,0:T(1,128)} %reshape.491), calls=%async_computation.1 | async-start | bytes 16384 | tf_op jit(solution)/shard_map/all_to_all | solution.py:129
  79.2 20.3 %all-to-all-start.2 = ((bf16[16,2,8192]{2,1,0:T(2,128)(2,1)}), bf16[16,2,8192]{2,1,0:T(2,128)(2,1)S(1)}, u32[]{:S(2)}, u32[]{:S(2)}) async-start(bf16[16,2,8192]{2,1,0:T(2,128)(2,1)} %reshape.493), calls=%async_computation.2 | async-start | bytes 1048576 | tf_op jit(solution)/shard_map/all_to_all | solution.py:119
